TPU v7x, 512 devices: a whole 4x4x16 slice. The times are simulated.
512 devices in a mesh: seq: 8 (over y, core), expert: 64 (over z, x).
Axes of the slice: x: 4, y: 4, z: 16, core: 2. Of those that a mesh axis runs over, the one named last changes fastest.
Arguments:
- tokens: bfloat16 [65536, 2048], P(('seq', 'expert')), may hold values from -4 to 4
- routes: int32 [65536, 8], P(('seq', 'expert')), may hold values from 0 to 127, all different within a row; in each aligned block of 128 rows (0 to 127, 128 to 255, ...) at most 16 rows name the same one
- gate_shares: int32 [65536, 8], P(('seq', 'expert')), may hold values from 1 to 65536
- gate_up: bfloat16 [128, 2048, 768], P('expert', 'seq'), may hold values from -0.125 to 0.125
Outputs:
- gram: float32 [128, 384, 384], P('expert', 'seq')
- maxima: float32 [128, 2048], P('expert', 'seq')
Inputs may be any that keep to these rules, and one draw needn't show every extreme that they name: `routes`: among the 128 rows of one device no expert is named more than 16 times.
All inputs are finite; a program needn't handle non-finite values.
Results may differ from a plain program's by a relative error of at most 0.0049.
Values may be sent and summed in bfloat16 or wider, within the bound.
A program may use at most 64 MiB of HBM per device.

v0:
```python
import jax
import jax.numpy as jnp
from jax import lax
from jax.sharding import PartitionSpec as P

D = 2048
FWIN = 384


def hidden_of(projected):
    return (jax.nn.silu(projected[..., :FWIN]) * projected[..., FWIN:]).astype(jnp.bfloat16)


def split_weighted(hidden, row_shares):
    weighted = hidden.astype(jnp.float32) * row_shares[..., None]
    weighted_high = weighted.astype(jnp.bfloat16)
    weighted_low = (weighted - weighted_high.astype(jnp.float32)).astype(jnp.bfloat16)
    return (weighted_high, weighted_low)


def body(tokens, routes, gate_shares, gate_up):
    tok_rows = tokens.shape[0]
    top_count = routes.shape[1]
    expert_count = lax.axis_size("expert")
    seq_count = lax.axis_size("seq")
    local_count = gate_up.shape[0]
    all_experts = local_count * expert_count
    capacity = 2 * tok_rows * top_count // all_experts
    norm_factor = all_experts / (tok_rows * seq_count * expert_count * top_count)
    chosen = routes.reshape(-1)
    shares = gate_shares.reshape(-1).astype(jnp.float32) / 65536.0
    one_hot = (chosen[:, None] == jnp.arange(all_experts, dtype=jnp.int32)[None, :]).astype(
        jnp.int32
    )
    ranked = jnp.sum((jnp.cumsum(one_hot, axis=0) - one_hot) * one_hot, axis=1)
    slot_index = chosen * capacity + ranked
    token_index = jnp.arange(tok_rows * top_count, dtype=jnp.int32) // top_count
    outgoing_rows = (
        jnp.zeros((all_experts * capacity, D), jnp.bfloat16).at[slot_index].set(tokens[token_index])
    )
    out_shares = jnp.zeros((all_experts * capacity,), jnp.float32).at[slot_index].set(shares)
    outgoing_rows = outgoing_rows.reshape(expert_count, local_count, capacity, D)
    out_shares = out_shares.reshape(expert_count, local_count, capacity)
    arrived, arrived_shares = (
        lax.all_to_all(outgoing_rows, "expert", split_axis=0, concat_axis=0, tiled=True),
        lax.all_to_all(
            out_shares.astype(jnp.bfloat16), "expert", split_axis=0, concat_axis=0, tiled=True
        ).astype(out_shares.dtype),
    )
    is_live = arrived_shares > 0.0
    channel_max = jnp.max(jnp.where(is_live[..., None], jnp.abs(arrived), 0), axis=(0, 2)).astype(
        jnp.float32
    )
    projected = jnp.einsum(
        "slcd,ldf->lscf",
        arrived,
        lax.all_gather(gate_up, "seq", axis=1, tiled=True),
        preferred_element_type=jnp.float32,
    )
    hidden = hidden_of(projected).reshape(local_count, expert_count * capacity, FWIN)
    row_shares = jnp.transpose(arrived_shares, (1, 0, 2)).reshape(
        local_count, expert_count * capacity
    )
    weighted_high, weighted_low = split_weighted(hidden, row_shares)
    gram_part = jnp.einsum(
        "lrf,lrg->lfg", hidden, weighted_high, preferred_element_type=jnp.float32
    )
    gram_part = gram_part + jnp.einsum(
        "lrf,lrg->lfg", hidden, weighted_low, preferred_element_type=jnp.float32
    )
    gram_part = gram_part * norm_factor
    gram = lax.psum_scatter(gram_part, "seq", scatter_dimension=1, tiled=True)
    full_max = lax.pmax(channel_max, "seq")
    slice_width = D // seq_count
    maxima = lax.dynamic_slice_in_dim(full_max, lax.axis_index("seq") * slice_width, slice_width, 1)
    return (gram, maxima)


def solution(mesh):
    return jax.shard_map(
        body,
        mesh=mesh,
        in_specs=(
            P(("seq", "expert"), None),
            P(("seq", "expert"), None),
            P(("seq", "expert"), None),
            P("expert", "seq", None),
        ),
        out_specs=(P("expert", "seq", None), P("expert", "seq")),
        check_vma=False,
    )
```

profile of v0, /device:TPU:1, one launch (start us, length us, event | category | flops | bytes accessed | tf_op | source)
XLA Modules:
  0.0 496.0 jit_solution(5624225172314754121)
XLA Ops:
  7.2 0.0 copy-start
  7.2 0.0 copy-start.1
  7.2 0.8 copy.20
  8.0 0.1 eq.29
  8.1 0.1 eq.25
  8.2 0.7 broadcast_multiply_fusion
  8.9 0.1 copy.22
  9.0 0.2 fusion.21
  9.3 0.1 copy.23
  9.4 0.1 copy.19
  9.5 0.1 mul.47
  9.6 0.0 copy-done.1
  9.6 0.1 copy.25
  9.7 0.1 reshape.130
  9.8 0.4 fusion.20
  10.2 4.3 scatter_custom_fusion.1
  14.6 0.7 convert_element_type.46
  15.3 19.3 %all-to-all-start.1 = ((bf16[64,2,16]{2,1,0:T(2,128)(2,1)}), bf16[64,2,16]{2,1,0:T(2,128)(2,1)S(1)}, u32[]{:S(2)}, u32[]{:S(2)}) async-start(bf16[64,2,16]{2,1,0:T(2,128)(2,1)} %convert_element_type.46), calls=%async_computation.1 | async-start | bytes 65536 | tf_op jit(solution)/shard_map/all_to_all | solution.py:46
  34.6 0.0 copy-done
  34.6 24.9 %scatter_custom_fusion = bf16[2048,2048]{1,0:T(8,128)(2,1)} fusion(s32[1024]{0:T(1024)S(1)} %bitcast.30, bf16[128,2048]{1,0:T(8,128)(2,1)S(1)} %copy-done, s32[1024]{0:T(1024)S(1)} %broadcast_clamp_fusion, bf16[]{:T(256)} %constant.19.clone.1), kind=kCustom, calls=%fused_computation.7 | custom fusion | bytes 8388610 | tf_op jit(solution)/shard_map/scatter | solution.py:39
  59.5 0.0 all-to-all-done.1
  59.5 14.6 %all-to-all-start = ((bf16[64,2,16,2048]{3,2,1,0:T(8,128)(2,1)}), bf16[64,2,16,2048]{3,2,1,0:T(8,128)(2,1)}, u32[]{:S(2)}, u32[]{:S(2)}) async-start(bf16[64,2,16,2048]{3,2,1,0:T(8,128)(2,1)} %bitcast.24), calls=%async_computation | async-start | bytes 16777216 | tf_op jit(solution)/shard_map/all_to_all | solution.py:45
  74.2 0.0 all-gather.2.cloned.1.call-start
  74.2 0.7 all-gather.2.cloned.1.call-update
  74.9 0.0 reduce-scatter.2.cloned.1.call-start
  75.0 0.1 mul.51
  75.1 52.8 %all-gather.2.cloned.1.call-done = bf16[2,2048,768]{2,1,0:T(8,128)(2,1)} async-done(((bf16[2,256,768]{2,1,0:T(8,128)(2,1)}), bf16[2,2048,768]{2,1,0:T(8,128)(2,1)}) %all-gather.2.cloned.1.call-update) | async-done | bytes 6291472 | tf_op jit(solution)/shard_map/all_gather | solution.py:57
  127.8 307.5 %all-to-all-done = bf16[64,2,16,2048]{3,2,1,0:T(8,128)(2,1)} async-done(((bf16[64,2,16,2048]{3,2,1,0:T(8,128)(2,1)}), bf16[64,2,16,2048]{3,2,1,0:T(8,128)(2,1)}, u32[]{:S(2)}, u32[]{:S(2)}) %all-to-all-start) | async-done | bytes 8388640 | tf_op jit(solution)/shard_map/all_to_all | solution.py:45
  435.4 10.0 %fusion = f32[2,64,16,768]{3,2,1,0:T(8,128)S(1)} fusion(bf16[64,2,16,2048]{3,2,1,0:T(8,128)(2,1)} %all-to-all-done, bf16[2,2048,768]{2,1,0:T(8,128)(2,1)} %all-gather.2.cloned.1.call-done), kind=kOutput, calls=%fused_computation.3 | convolution fusion | flops 6442450944 | bytes 20971520 | tf_op jit(solution)/shard_map/slcd,ldf->lscf/dot_general | solution.py:54
  445.4 0.9 fusion.6
  446.3 1.2 fusion.10
  447.6 2.3 fusion.16
  449.9 0.0 reduce-scatter.2.cloned.1.call-update
  450.0 5.2 %select_reduce_fusion = bf16[2,2048]{1,0:T(2,128)(2,1)S(1)} fusion(bf16[64,2,16,2048]{3,2,1,0:T(8,128)(2,1)} %all-to-all-done, pred[64,2,16]{2,1,0:T(4,128)(4,1)S(1)} %convert_compare_fusion), kind=kLoop, calls=%fused_computation.5 | loop fusion | flops 12578816 | bytes 8398848 | tf_op jit(solution)/shard_map/reduce_max | solution.py:51
  455.2 29.8 %pmax.7 = f32[2,2048]{1,0:T(2,128)S(1)} all-reduce(bf16[2,2048]{1,0:T(2,128)(2,1)S(1)} %select_reduce_fusion), channel_id=1, replica_groups=mesh['seq'=8,'expert'=64] {'seq'}, use_global_device_ids=true, to_apply=%region_7.8 | all-reduce | flops 4096 | bytes 24576 | tf_op jit(solution)/shard_map/pmax | solution.py:73
  485.0 0.6 constant_dynamic-slice_fusion
  485.6 3.5 reduce-scatter.2.cloned.1.call-done
  (12 shorter events, 0.2 us)
Async XLA Ops:
  7.2 27.4 %copy-start = (bf16[128,2048]{1,0:T(8,128)(2,1)S(1)}, bf16[128,2048]{1,0:T(8,128)(2,1)}, u32[]{:S(2)}) copy-start(bf16[128,2048]{1,0:T(8,128)(2,1)} %param.4) | copy-start | bytes 1572868
  7.2 2.4 copy-start.1
  15.3 44.3 %all-to-all-start.1 = ((bf16[64,2,16]{2,1,0:T(2,128)(2,1)}), bf16[64,2,16]{2,1,0:T(2,128)(2,1)S(1)}, u32[]{:S(2)}, u32[]{:S(2)}) async-start(bf16[64,2,16]{2,1,0:T(2,128)(2,1)} %convert_element_type.46), calls=%async_computation.1 | async-start | bytes 65536 | tf_op jit(solution)/shard_map/all_to_all | solution.py:46
  59.5 375.9 %all-to-all-start = ((bf16[64,2,16,2048]{3,2,1,0:T(8,128)(2,1)}), bf16[64,2,16,2048]{3,2,1,0:T(8,128)(2,1)}, u32[]{:S(2)}, u32[]{:S(2)}) async-start(bf16[64,2,16,2048]{3,2,1,0:T(8,128)(2,1)} %bitcast.24), calls=%async_computation | async-start | bytes 16777216 | tf_op jit(solution)/shard_map/all_to_all | solution.py:45
  74.2 53.7 %all-gather.2.cloned.1.call-start = ((), (), s32[]{:S(2)}) async-start(), calls=%async_computation.3 | async-start | bytes 7077888 | tf_op jit(solution)/shard_map/all_gather | solution.py:57
  74.9 414.2 %reduce-scatter.2.cloned.1.call-start = ((), (), s32[]{:S(2)}) async-start(), calls=%async_computation.4 | async-start | bytes 1327104 | tf_op jit(solution)/shard_map/reduce_scatter | solution.py:72
Sparse Core Ops, SparseCore 0:
  77.1 50.7 all-gather.1
  450.0 39.0 reduce-scatter.1
where the time goes:
time: 497 us; the launch traced here: 496 us
  waiting for transfers between devices  365 us (73%)
  starting transfers between devices  34 us (7%)
  local copies, waits for them, and re-layouts  32.3 us (6%)
  blocking collectives  29.8 us (6%)
  between operations  14.2 us (3%)
  matrix products  13.6 us (3%)
  other arithmetic  7.54 us (2%)
    all_to_all x1, waiting for transfers between devices, body(): lax.all_to_all(outgoing_rows, 'expert', split_axis=0, concat_axis=0, tile...  308 us
    all_gather x1, waiting for transfers between devices, body(): lax.all_gather(gate_up, 'seq', axis=1, tiled=True)  52.8 us
    pmax x1, blocking collectives, body(): full_max = lax.pmax(channel_max, 'seq')  29.8 us
    scatter x1, local copies, waits for them, and re-layouts, body(): jnp.zeros((all_experts * capacity, D), jnp.bfloat16).at[slot_index]  24.9 us
    all_to_all x1, starting transfers between devices, body(): lax.all_to_all(out_shares.astype(jnp.bfloat16), 'expert', split_axis=0, c...  19.3 us
    all_to_all x1, starting transfers between devices, body(): lax.all_to_all(outgoing_rows, 'expert', split_axis=0, concat_axis=0, tile...  14.6 us
    dot_general x1, matrix products, body(): jnp.einsum('slcd,ldf->lscf', arrived, lax.all_gather(gate_up, 'seq', axis...  10 us
  transfers between devices with their start and end apart: 4, of which 3 were waited for; matrix products, arithmetic and copies ran while one was open for 6% of the time, Pallas kernels for 0%

commit v1 on v0

v1 whole, which is shorter than its diff:
```python
import functools

import jax
import jax.numpy as jnp
from jax import lax
from jax.experimental import pallas as pl
from jax.experimental.pallas import tpu as pltpu
from jax.sharding import PartitionSpec as P

NX, NY, NZ = 4, 4, 16
BLK = 128
TOP = 8
CAP = 16
D = 2048
FWIN = 384
EXPERTS = 128
HOPS = NZ // 2
HALF = BLK // 2
DSEQ = D // (2 * NY)
NB = 2 * NZ
ROWS = NB * CAP
MESH = pl.DeviceIdType.MESH
NORM = EXPERTS / (BLK * 2 * NY * NX * NZ * TOP)
F32 = jnp.float32
BF16 = jnp.bfloat16


def kernel(
    tok, meta, wgt, gram_out, max_out,
    toks, metas, picked, row_share, peak, weights, upper, proj, hid, wtd,
    part, own_part, part_max, got_x, got_x_max, slices, slice_max, got_y, got_y_max,
    loc_sem, ring_s, ring_r, rmeta_s, rmeta_r, mate_s, mate_r, mmeta_s, mmeta_r,
    swap_s, swap_r, first_s, first_r, frel_s, frel_r, sec_s, sec_r, srel_s, srel_r,
    gx_s, gx_r, mx_s, mx_r, gy_s, gy_r, my_s, my_r,
):
    seq = lax.axis_index("seq")
    exp = lax.axis_index("expert")
    y, c = seq // 2, seq % 2
    z, x = exp // NX, exp % NX
    mate_c = 1 - c

    def dev(dx=0, dy=0, dz=0, core=c):
        return ((y + dy) % NY * 2 + core, (z + dz) % NZ * NX + (x + dx) % NX)

    def send(src, dst, ss, rs, to):
        return pltpu.make_async_remote_copy(
            src_ref=src, dst_ref=dst, send_sem=ss, recv_sem=rs, device_id=to, device_id_type=MESH
        )

    barrier = pltpu.get_barrier_semaphore()
    peers = [dev(dz=1), dev(dz=-1), dev(core=mate_c)]
    peers += [dev(dx=k) for k in range(1, NX)]
    peers += [dev(dy=k, core=q) for k in range(1, NY) for q in (c, mate_c)]
    for peer in peers:
        pl.semaphore_signal(barrier, inc=1, device_id=peer, device_id_type=MESH)
    pl.semaphore_wait(barrier, len(peers))

    def origin(d, s):
        return (z - s) % NZ if d == 0 else (z + s) % NZ

    def rows_of(h):
        return pl.ds(h * HALF, HALF)

    def ring(d, s, h, o, src=None):
        there = toks.at[c, o, rows_of(h)]
        return send(there if src is None else src, there, ring_s.at[d, s, h], ring_r.at[d, s, h],
                    dev(dz=1 - 2 * d))

    def ring_meta(d, s, o, src=None):
        there = metas.at[c, o]
        return send(there if src is None else src, there, rmeta_s.at[d, s], rmeta_r.at[d, s],
                    dev(dz=1 - 2 * d))

    def mate(owner, s, d, o, part_rows=None, src=None):
        there = toks.at[owner, o] if part_rows is None else toks.at[owner, o, part_rows]
        return send(there if src is None else src, there, mate_s.at[s, d], mate_r.at[s, d],
                    dev(core=mate_c))

    def mate_meta(owner, s, d, o, src=None):
        there = metas.at[owner, o]
        return send(there if src is None else src, there, mmeta_s.at[s, d], mmeta_r.at[s, d],
                    dev(core=mate_c))

    def first_dev(step):
        return dev(dx=step * (1 - c), dy=step * c)

    def second_dev(step):
        return dev(dx=step * c, dy=step * (1 - c))

    def unit(df, ds, sl=None):
        xi = (x + df * (1 - c) + ds * c) % NX
        yi = (y + df * c + ds * (1 - c)) % NY
        if sl is None:
            return weights.at[xi, pl.ds(pl.multiple_of(yi * 2 * DSEQ, 2 * DSEQ), 2 * DSEQ)]
        return weights.at[xi, pl.ds(pl.multiple_of((yi * 2 + sl) * DSEQ, DSEQ), DSEQ)]

    def first(d, df):
        return send(unit(df, 0), unit(df, 0), first_s.at[d], first_r.at[d], first_dev(1 - 2 * d))

    def first_relay(d, df):
        return send(unit(df, 0, d), unit(df, 0, d), frel_s.at[d], frel_r.at[d],
                    first_dev(1 - 2 * d))

    def second(k, d, df, ds):
        return send(unit(df, ds), unit(df, ds), sec_s.at[k, d], sec_r.at[k, d],
                    second_dev(1 - 2 * d))

    def second_relay(k, d, df, ds):
        return send(unit(df, ds, d), unit(df, ds, d), srel_s.at[k, d], srel_r.at[k, d],
                    second_dev(1 - 2 * d))

    places = (0, -1, 1, 2)
    sides = (-1, 1)

    own_w = unit(0, 0, c)
    local = [
        pltpu.make_async_copy(tok, toks.at[c, z], loc_sem.at[0]),
        pltpu.make_async_copy(meta, metas.at[c, z], loc_sem.at[1]),
        pltpu.make_async_copy(wgt.at[c], own_w, loc_sem.at[2]),
    ]
    swap = send(wgt.at[mate_c], own_w, swap_s, swap_r, dev(core=mate_c))
    for d in (0, 1):
        ring_meta(d, 0, z, meta).start()
        for h in (0, 1):
            ring(d, 0, h, z, tok.at[rows_of(h)]).start()
    swap.start()
    for copy in local:
        copy.start()
    mate_meta(c, 0, 0, z, meta).start()
    mate(c, 0, 0, z, None, tok).start()

    lanes = lax.broadcasted_iota(jnp.int32, (BLK, BLK), 1)
    subs = lax.broadcasted_iota(jnp.int32, (BLK, BLK), 0)
    upper[...] = jnp.where(subs < lanes, 1.0, 0.0).astype(BF16)
    peak[...] = jnp.zeros_like(peak)

    local[2].wait()
    send(wgt.at[mate_c], unit(0, 0, mate_c), swap_s, swap_r, dev(core=mate_c)).wait_recv()
    for d in (0, 1):
        first(d, 0).start()
        second(0, d, 0, 0).start()

    slot = lax.broadcasted_iota(jnp.int32, (CAP, BLK), 0).astype(F32)
    expert_id = (z * 2 * NX + c + 2 * lax.broadcasted_iota(jnp.int32, (8, BLK), 0)).astype(F32)

    def pick(owner, o, b):
        info = metas[owner, o]
        named = jnp.zeros((8, BLK), F32)
        share = jnp.zeros((8, BLK), F32)
        for k in range(TOP):
            same = info[k : k + 1, :] == expert_id
            named = jnp.where(same, 1.0, named)
            share = jnp.where(same, info[TOP + k : TOP + k + 1, :], share)
        rank = jnp.dot(named.astype(BF16), upper[...], preferred_element_type=F32)
        rank = jnp.where(named > 0.5, rank, -1.0)
        at = pl.ds(pl.multiple_of(b * CAP, CAP), CAP)
        chosen = []
        for j in range(NX):
            one = jnp.where(rank[j : j + 1, :] == slot, 1.0, 0.0)
            chosen.append(one)
            col = jnp.sum(one * share[j : j + 1, :], axis=1, keepdims=True) * (1.0 / 65536.0)
            row_share[j, at, :] = jnp.broadcast_to(col, (CAP, BLK))
        chosen = jnp.concatenate(chosen, axis=0).astype(BF16)
        for n in range(0, D, 512):
            got = jnp.dot(chosen, toks[owner, o, :, n : n + 512], preferred_element_type=F32)
            picked_rows = got.astype(BF16)
            size = jnp.abs(got)
            for j in range(NX):
                picked[j, at, n : n + 512] = picked_rows[j * CAP : (j + 1) * CAP]
                both = jnp.maximum(size[j * CAP : j * CAP + 8], size[j * CAP + 8 : (j + 1) * CAP])
                peak[j, :, n : n + 512] = jnp.maximum(peak[j, :, n : n + 512], both)

    local[0].wait()
    local[1].wait()
    pick(c, z, 0)
    mate_meta(mate_c, 0, 0, z).wait_recv()
    mate(mate_c, 0, 0, z).wait_recv()
    pick(mate_c, z, 1)

    def mate_picks(s):
        for d in (0, 1):
            o = origin(d, s)
            mate_meta(mate_c, s, d, o).wait_recv()
            mate(mate_c, s, d, o).wait_recv()
            pick(mate_c, o, 4 * s + d)

    def ring_step(s, carry):
        for h in (0, 1):
            for d in (0, 1):
                o = origin(d, s)
                if h == 0:
                    ring_meta(d, s - 1, o).wait_recv()

                    @pl.when((s < HOPS - 1) | (d == 0))
                    def _():
                        ring_meta(d, s, o).start()

                    mate_meta(c, s, d, o).start()
                ring(d, s - 1, h, o).wait_recv()

                @pl.when((s < HOPS - 1) | (d == h))
                def _():
                    ring(d, s, h, o).start()

                if h == 1:
                    mate(c, s, d, o).start()

        @pl.when(s == 2)
        def _():
            for d in (0, 1):
                first(d, sides[d]).wait_recv()
                first_relay(d, sides[d]).start()
            for k in (1, 2):
                for d in (0, 1):
                    second(k, d, places[k], 0).start()

        @pl.when(s == 3)
        def _():
            for d in (0, 1):
                first_relay(d, 2).wait_recv()
                second(0, d, 0, sides[d]).wait_recv()
                second_relay(0, d, 0, sides[d]).start()
            for d in (0, 1):
                second(3, d, 2, 0).start()

        @pl.when(s == 4)
        def _():
            for k in (1, 2):
                for d in (0, 1):
                    second(k, d, places[k], sides[d]).wait_recv()
                    second_relay(k, d, places[k], sides[d]).start()

        @pl.when(s == 5)
        def _():
            for d in (0, 1):
                second(3, d, 2, sides[d]).wait_recv()
                second_relay(3, d, 2, sides[d]).start()

        for d in (0, 1):
            pick(c, origin(d, s), 4 * s - 2 + d)

        @pl.when(s >= 2)
        def _():
            mate_picks(s - 1)

        return carry

    lax.fori_loop(1, HOPS, ring_step, 0)

    far = (z + HOPS) % NZ
    last = HOPS - 1
    ring_meta(0, last, far).wait_recv()
    mate_meta(c, HOPS, 0, far).start()
    for d in (0, 1):
        ring(d, last, d, far).wait_recv()
        mate(c, HOPS, d, far, rows_of(d)).start()
    mate_picks(last)
    pick(c, far, NB - 2)
    for k in range(4):
        for d in (0, 1):
            second_relay(k, d, places[k], 2).wait_recv()
    mate_meta(mate_c, HOPS, 0, far).wait_recv()
    for d in (0, 1):
        mate(mate_c, HOPS, d, far, rows_of(d)).wait_recv()
    pick(mate_c, far, NB - 1)

    def to_x(i):
        return (
            send(part.at[i], got_x.at[i], gx_s.at[i], gx_r.at[i], dev(dx=i + 1)),
            send(part_max.at[i], got_x_max.at[i], mx_s.at[i], mx_r.at[i], dev(dx=i + 1)),
        )

    def one_expert(i, carry):
        j = (x + i + 1) % NX

        def tile(t, carry):
            m = pl.ds(pl.multiple_of((t // 3) * 256, 256), 256)
            n = pl.ds(pl.multiple_of((t % 3) * 256, 256), 256)
            proj[m, n] = jnp.dot(picked[j, m, :], weights[j, :, n], preferred_element_type=F32)
            return carry

        lax.fori_loop(0, 2 * ROWS // 512 * 3, tile, 0)

        @pl.when(i > 0)
        def _():
            for copy in to_x(i - 1):
                copy.start()

        def gate(t, carry):
            m = pl.ds(pl.multiple_of(t * 64, 64), 64)
            g = proj[m, 0:FWIN]
            h = (g / (1.0 + jnp.exp(-g)) * proj[m, FWIN : 2 * FWIN]).astype(BF16)
            s = row_share[j, m, :]
            w = h.astype(F32) * jnp.concatenate([s] * (FWIN // BLK), axis=1)
            high = w.astype(BF16)
            hid[m, :] = h
            wtd[m, 0:FWIN] = high
            wtd[m, FWIN : 2 * FWIN] = (w - high.astype(F32)).astype(BF16)
            return carry

        lax.fori_loop(0, ROWS // 64, gate, 0)
        over_rows = (((0,), (0,)), ((), ()))
        g = lax.dot_general(hid[...], wtd[:, 0:FWIN], over_rows, preferred_element_type=F32)
        g = g + lax.dot_general(
            hid[...], wtd[:, FWIN : 2 * FWIN], over_rows, preferred_element_type=F32
        )
        top = jnp.max(peak[j], axis=0, keepdims=True)
        for r in range(D // BLK):
            part_max[i, r : r + 1, :] = top[:, r * BLK : (r + 1) * BLK]

        @pl.when(i < NX - 1)
        def _():
            part[i] = g.astype(BF16)

        @pl.when(i == NX - 1)
        def _():
            own_part[...] = g

        return carry

    lax.fori_loop(0, NX, one_expert, 0)

    for i in range(NX - 1):
        for copy in to_x(i):
            copy.wait_recv()
    slice_max[...] = jnp.maximum(
        jnp.maximum(part_max[NX - 1], got_x_max[0]), jnp.maximum(got_x_max[1], got_x_max[2])
    )
    width = FWIN // (2 * NY)
    for q in range(2 * NY):
        at = pl.ds(q * width, width)
        total = own_part[at, :]
        for i in range(NX - 1):
            total = total + got_x[i, at, :].astype(F32)
        slices[q] = total.astype(BF16)
    got_y[c, y] = slices[seq]
    got_y_max[c, y] = slice_max[...]

    def to_y(k):
        dy, core = k // 2, (c if k % 2 == 0 else mate_c)
        to = dev(dy=dy, core=core)
        return (
            send(slices.at[to[0]], got_y.at[c, y], gy_s.at[k - 1], gy_r.at[k - 1], to),
            send(slice_max, got_y_max.at[c, y], my_s.at[k - 1], my_r.at[k - 1], to),
        )

    def from_y(k):
        dy, core = k // 2, (c if k % 2 == 0 else mate_c)
        src_y = (y - dy) % NY
        to = dev(dy=dy, core=core)
        return (
            send(slices.at[to[0]], got_y.at[core, src_y], gy_s.at[k - 1], gy_r.at[k - 1], to),
            send(slice_max, got_y_max.at[core, src_y], my_s.at[k - 1], my_r.at[k - 1], to),
        )

    for k in range(1, 2 * NY):
        for copy in to_y(k):
            copy.start()

    for d in (0, 1):
        first(d, 0).wait_send()
        first_relay(d, sides[d]).wait_send()
        for k in range(4):
            second(k, d, places[k], 0).wait_send()
            second_relay(k, d, places[k], sides[d]).wait_send()
    swap.wait_send()
    mate_meta(c, 0, 0, z, meta).wait_send()
    mate(c, 0, 0, z, None, tok).wait_send()
    for d in (0, 1):
        ring_meta(d, 0, z, meta).wait_send()
        for h in (0, 1):
            ring(d, 0, h, z, tok.at[rows_of(h)]).wait_send()

    def drain(s, carry):
        for d in (0, 1):
            o = origin(d, s)
            mate_meta(c, s, d, o).wait_send()
            mate(c, s, d, o).wait_send()

            @pl.when((s < HOPS - 1) | (d == 0))
            def _():
                ring_meta(d, s, o).wait_send()

            for h in (0, 1):

                @pl.when((s < HOPS - 1) | (d == h))
                def _():
                    ring(d, s, h, o).wait_send()

        return carry

    lax.fori_loop(1, HOPS, drain, 0)
    mate_meta(c, HOPS, 0, far).wait_send()
    for d in (0, 1):
        mate(c, HOPS, d, far, rows_of(d)).wait_send()
    for i in range(NX - 1):
        for copy in to_x(i):
            copy.wait_send()

    for k in range(1, 2 * NY):
        for copy in from_y(k):
            copy.wait_recv()
    row = lax.broadcasted_iota(jnp.int32, (D // BLK, BLK), 0)
    for p in (0, 1):
        total = got_y[p, 0].astype(F32)
        top = got_y_max[p, 0]
        for k in range(1, NY):
            total = total + got_y[p, k].astype(F32)
            top = jnp.maximum(top, got_y_max[p, k])
        gram_out[p] = total * NORM
        for r in (0, 1):
            here = jnp.where(row == 2 * seq + r, top, 0.0)
            max_out[p : p + 1, r * BLK : (r + 1) * BLK] = jnp.max(here, axis=0, keepdims=True)
    for k in range(1, 2 * NY):
        for copy in to_y(k):
            copy.wait_send()


def body(tokens, routes, gate_shares, gate_up):
    meta = jnp.concatenate([routes.T, gate_shares.T], axis=0).astype(F32)
    dma = pltpu.SemaphoreType.DMA
    width = FWIN // (2 * NY)
    pairs = [
        (2, HOPS, 2), (2, HOPS), (HOPS + 1, 2), (HOPS + 1, 2), (), (2,), (2,), (4, 2), (4, 2),
        (NX - 1,), (NX - 1,), (2 * NY - 1,), (2 * NY - 1,),
    ]
    sems = [dma((3,))]
    for shape in pairs:
        sems += [dma(shape), dma(shape)]
    return pl.pallas_call(
        kernel,
        out_shape=(
            jax.ShapeDtypeStruct((2, width, FWIN), F32),
            jax.ShapeDtypeStruct((2, D // (2 * NY)), F32),
        ),
        in_specs=[pl.BlockSpec(memory_space=pl.ANY)] * 3,
        out_specs=(
            pl.BlockSpec(memory_space=pltpu.VMEM),
            pl.BlockSpec(memory_space=pltpu.VMEM),
        ),
        scratch_shapes=[
            pltpu.VMEM((2, NZ, BLK, D), BF16),
            pltpu.VMEM((2, NZ, 2 * TOP, BLK), F32),
            pltpu.VMEM((NX, ROWS, D), BF16),
            pltpu.VMEM((NX, ROWS, BLK), F32),
            pltpu.VMEM((NX, 8, D), F32),
            pltpu.VMEM((NX, D, 2 * FWIN), BF16),
            pltpu.VMEM((BLK, BLK), BF16),
            pltpu.VMEM((ROWS, 2 * FWIN), F32),
            pltpu.VMEM((ROWS, FWIN), BF16),
            pltpu.VMEM((ROWS, 2 * FWIN), BF16),
            pltpu.VMEM((NX - 1, FWIN, FWIN), BF16),
            pltpu.VMEM((FWIN, FWIN), F32),
            pltpu.VMEM((NX, D // BLK, BLK), F32),
            pltpu.VMEM((NX - 1, FWIN, FWIN), BF16),
            pltpu.VMEM((NX - 1, D // BLK, BLK), F32),
            pltpu.VMEM((2 * NY, width, FWIN), BF16),
            pltpu.VMEM((D // BLK, BLK), F32),
            pltpu.VMEM((2, NY, width, FWIN), BF16),
            pltpu.VMEM((2, NY, D // BLK, BLK), F32),
            *sems,
        ],
        compiler_params=pltpu.CompilerParams(
            collective_id=0, has_side_effects=True, vmem_limit_bytes=60 * 1024 * 1024
        ),
    )(tokens, meta, gate_up)


def solution(mesh):
    return jax.shard_map(
        body,
        mesh=mesh,
        in_specs=(
            P(("seq", "expert"), None),
            P(("seq", "expert"), None),
            P(("seq", "expert"), None),
            P("expert", "seq", None),
        ),
        out_specs=(P("expert", "seq", None), P("expert", "seq")),
        check_vma=False,
    )
```

time: 497 us -> 142 us (0.29)
  waiting for transfers between devices: 365 us -> 0 us
  Pallas kernels: 0 us -> 138 us
  starting transfers between devices: 34 us -> 0 us
  local copies, waits for them, and re-layouts: 32.3 us -> 2.16 us
  blocking collectives: 29.8 us -> 0 us
  matrix products: 13.6 us -> 0 us
  between operations: 14.2 us -> 0.65 us
  other arithmetic: 7.54 us -> 1.3 us
    all_to_all x2 -> x0, waiting for transfers between devices: 308 us -> none  [the longest x1 308 us: body(): lax.all_to_all(outgoing_rows, 'expert', split_axis=0, concat_axis=0, tile...]
    pallas_call x0 -> x1, Pallas kernels: none -> 138 us  [body(): pl.pallas_call(kernel, out_shape=(jax.ShapeDtypeStruct((2, width, FWIN),...]
    all_gather x1 -> x0, waiting for transfers between devices: 52.8 us -> none  [body(): lax.all_gather(gate_up, 'seq', axis=1, tiled=True)]
    all_to_all x2 -> x0, starting transfers between devices: 33.9 us -> none  [the longest x1 19.3 us: body(): lax.all_to_all(out_shares.astype(jnp.bfloat16), 'expert', split_axis=0, c...]
    pmax x1 -> x0, blocking collectives: 29.8 us -> none  [body(): full_max = lax.pmax(channel_max, 'seq')]
    scatter x2 -> x0, local copies, waits for them, and re-layouts: 29.3 us -> none  [the longest x1 24.9 us: body(): jnp.zeros((all_experts * capacity, D), jnp.bfloat16).at[slot_index]]
    dot_general x3 -> x0, matrix products: 13.6 us -> none  [the longest x1 10 us: body(): jnp.einsum('slcd,ldf->lscf', arrived, lax.all_gather(gate_up, 'seq', axis...]
    reduce_max x1 -> x0, other arithmetic: 5.18 us -> none  [body(): jnp.max(jnp.where(is_live[..., None], jnp.abs(arrived), 0), axis=(0, 2))]
  transfers between devices with their start and end apart: 4 -> 0, of which waited for: 3 -> 0; matrix products, arithmetic and copies ran while one was open for 6% -> 0% of each run, Pallas kernels for 0% -> 0%
where the time goes in v1:
time: 142 us
  Pallas kernels  138 us (97%)
  local copies, waits for them, and re-layouts  2.16 us (2%)
    pallas_call x1, Pallas kernels, body(): pl.pallas_call(kernel, out_shape=(jax.ShapeDtypeStruct((2, width, FWIN),...  138 us

profile of v1, /device:TPU:1, one launch (start us, length us, event | category | flops | bytes accessed | tf_op | source)
XLA Modules:
  0.0 142.3 jit_solution(12559272819689718629)
XLA Ops:
  0.6 1.3 add_convert_fusion.meta
  1.9 138.1 %shard_map.59 = (f32[2,48,384]{2,1,0:T(8,128)}, f32[2,256]{1,0:T(2,128)}) custom-call(bf16[128,2048]{1,0:T(8,128)(2,1)} %tok.1, f32[16,128]{1,0:T(8,128)} %add_convert_fusion.meta, bf16[2,256,768]{2,1,0:T(8,128)(2,1)} %wgt.1), custom_call_target="tpu_custom_call" | custom-call | tf_op jit(solution)/shard_map/pallas_call | solution.py:430
  140.1 0.0 copy-start
  140.1 1.6 %copy.8 = f32[2,48,384]{2,1,0:T(8,128)} copy(f32[2,48,384]{2,1,0:T(8,128)} %get-tuple-element.4) | data formatting | bytes 294912
  141.7 0.0 copy-done
  141.7 0.6 copy.9
Async XLA Ops:
  140.1 1.6 %copy-start = (f32[2,256]{1,0:T(2,128)S(1)}, f32[2,256]{1,0:T(2,128)}, u32[]{:S(2)}) copy-start(f32[2,256]{1,0:T(2,128)} %get-tuple-element.5) | copy-start | bytes 6148

commit v2 on v1

v2 whole, which is shorter than its diff:
```python
import functools

import jax
import jax.numpy as jnp
from jax import lax
from jax.experimental import pallas as pl
from jax.experimental.pallas import tpu as pltpu
from jax.sharding import PartitionSpec as P

NX, NY, NZ = 4, 4, 16
BLK = 128
TOP = 8
CAP = 16
D = 2048
FWIN = 384
EXPERTS = 128
HOPS = NZ // 2
NH = 2
PIECE = BLK // NH
DSEQ = D // (2 * NY)
NB = 2 * NZ
ROWS = NB * CAP
EARLY = (256, 384)
MESH = pl.DeviceIdType.MESH
NORM = EXPERTS / (BLK * 2 * NY * NX * NZ * TOP)
F32 = jnp.float32
BF16 = jnp.bfloat16


def kernel(
    tok, routes, shares, wgt, gram_out, max_out,
    toks, metas, picked, row_share, peak, weights, upper, proj, hid, wtd,
    gram, part, part_max, got_1, got_x_max, slices, slice_max, got_2, got_y_max,
    loc_sem, ring_s, ring_r, rmeta_s, rmeta_r, mate_s, mate_r, mmeta_s, mmeta_r,
    swap_s, swap_r, first_s, first_r, frel_s, frel_r, sec_s, sec_r, srel_s, srel_r,
    g1_s, g1_r, p1_s, p1_r, mx_s, mx_r, g2_s, g2_r, my_s, my_r,
):
    seq = lax.axis_index("seq")
    exp = lax.axis_index("expert")
    y, c = seq // 2, seq % 2
    z, x = exp // NX, exp % NX
    mate_c = 1 - c

    def dev(dx=0, dy=0, dz=0, core=c):
        return ((y + dy) % NY * 2 + core, (z + dz) % NZ * NX + (x + dx) % NX)

    def send(src, dst, ss, rs, to):
        return pltpu.make_async_remote_copy(
            src_ref=src, dst_ref=dst, send_sem=ss, recv_sem=rs, device_id=to, device_id_type=MESH
        )

    barrier = pltpu.get_barrier_semaphore()
    peers = [dev(dz=1), dev(dz=-1), dev(core=mate_c)]
    peers += [dev(dx=k, core=q) for k in range(1, NX) for q in (c, mate_c)]
    peers += [dev(dy=k, core=q) for k in range(1, NY) for q in (c, mate_c)]
    for peer in peers:
        pl.semaphore_signal(barrier, inc=1, device_id=peer, device_id_type=MESH)
    own_rows = pl.ds(pl.multiple_of((y * 2 + c) * DSEQ, DSEQ), DSEQ)
    local = [
        pltpu.make_async_copy(routes, metas.at[c, z, 0:TOP], loc_sem.at[0]),
        pltpu.make_async_copy(shares, metas.at[c, z, TOP : 2 * TOP], loc_sem.at[1]),
        pltpu.make_async_copy(wgt.at[c], weights.at[x, own_rows], loc_sem.at[2]),
        pltpu.make_async_copy(tok, toks.at[c, z], loc_sem.at[3]),
    ]
    for copy in local:
        copy.start()
    lanes = lax.broadcasted_iota(jnp.int32, (BLK, BLK), 1)
    subs = lax.broadcasted_iota(jnp.int32, (BLK, BLK), 0)
    upper[...] = jnp.where(subs < lanes, 1.0, 0.0).astype(BF16)
    peak[...] = jnp.zeros_like(peak)
    pl.semaphore_wait(barrier, len(peers))

    def origin(d, s):
        return (z - s) % NZ if d == 0 else (z + s) % NZ

    def rows_of(h):
        return pl.ds(h * PIECE, PIECE)

    def ring(d, s, h, o, src=None):
        there = toks.at[c, o, rows_of(h)]
        return send(there if src is None else src, there, ring_s.at[d, s, h], ring_r.at[d, s, h],
                    dev(dz=1 - 2 * d))

    def ring_meta(d, s, o, src=None):
        there = metas.at[c, o]
        return send(there if src is None else src, there, rmeta_s.at[d, s], rmeta_r.at[d, s],
                    dev(dz=1 - 2 * d))

    def mate(owner, s, d, o, part_rows=None, src=None):
        there = toks.at[owner, o] if part_rows is None else toks.at[owner, o, part_rows]
        return send(there if src is None else src, there, mate_s.at[s, d], mate_r.at[s, d],
                    dev(core=mate_c))

    def mate_meta(owner, s, d, o, src=None):
        there = metas.at[owner, o]
        return send(there if src is None else src, there, mmeta_s.at[s, d], mmeta_r.at[s, d],
                    dev(core=mate_c))

    def first_dev(step):
        return dev(dx=step * (1 - c), dy=step * c)

    def second_dev(step):
        return dev(dx=step * c, dy=step * (1 - c))

    def unit(df, ds, sl=None):
        xi = (x + df * (1 - c) + ds * c) % NX
        yi = (y + df * c + ds * (1 - c)) % NY
        if sl is None:
            return weights.at[xi, pl.ds(pl.multiple_of(yi * 2 * DSEQ, 2 * DSEQ), 2 * DSEQ)]
        return weights.at[xi, pl.ds(pl.multiple_of((yi * 2 + sl) * DSEQ, DSEQ), DSEQ)]

    def first(d, df):
        return send(unit(df, 0), unit(df, 0), first_s.at[d], first_r.at[d], first_dev(1 - 2 * d))

    def first_relay(d, df):
        return send(unit(df, 0, d), unit(df, 0, d), frel_s.at[d], frel_r.at[d],
                    first_dev(1 - 2 * d))

    def second(k, d, df, ds):
        return send(unit(df, ds), unit(df, ds), sec_s.at[k, d], sec_r.at[k, d],
                    second_dev(1 - 2 * d))

    def second_relay(k, d, df, ds):
        return send(unit(df, ds, d), unit(df, ds, d), srel_s.at[k, d], srel_r.at[k, d],
                    second_dev(1 - 2 * d))

    places = (0, -1, 1, 2)
    sides = (-1, 1)

    swap = send(wgt.at[mate_c], weights.at[x, own_rows], swap_s, swap_r, dev(core=mate_c))
    for d in (0, 1):
        for h in range(NH):
            ring(d, 0, h, z, tok.at[rows_of(h)]).start()
    swap.start()
    local[0].wait()
    local[1].wait()
    for d in (0, 1):
        ring_meta(d, 0, z).start()
    mate_meta(c, 0, 0, z).start()
    mate(c, 0, 0, z, None, tok).start()

    local[2].wait()
    send(wgt.at[mate_c], unit(0, 0, mate_c), swap_s, swap_r, dev(core=mate_c)).wait_recv()
    for d in (0, 1):
        first(d, 0).start()
        second(0, d, 0, 0).start()

    slot = lax.broadcasted_iota(jnp.int32, (CAP, BLK), 0).astype(F32)
    expert_id = z * 2 * NX + c + 2 * lax.broadcasted_iota(jnp.int32, (8, BLK), 0)

    def pick(owner, o, b):
        info = metas[owner, o]
        named = jnp.zeros((8, BLK), F32)
        share = jnp.zeros((8, BLK), jnp.int32)
        for k in range(TOP):
            same = info[k : k + 1, :] == expert_id
            named = jnp.where(same, 1.0, named)
            share = jnp.where(same, info[TOP + k : TOP + k + 1, :], share)
        share = share.astype(F32)
        rank = jnp.dot(named.astype(BF16), upper[...], preferred_element_type=F32)
        rank = jnp.where(named > 0.5, rank, -1.0)
        at = pl.ds(pl.multiple_of(b * CAP, CAP), CAP)
        chosen = []
        for j in range(NX):
            one = jnp.where(rank[j : j + 1, :] == slot, 1.0, 0.0)
            chosen.append(one)
            col = jnp.sum(one * share[j : j + 1, :], axis=1, keepdims=True) * (1.0 / 65536.0)
            row_share[j, at, :] = jnp.broadcast_to(col, (CAP, BLK))
        chosen = jnp.concatenate(chosen, axis=0).astype(BF16)
        for n in range(0, D, 512):
            got = jnp.dot(chosen, toks[owner, o, :, n : n + 512], preferred_element_type=F32)
            picked_rows = got.astype(BF16)
            size = jnp.abs(got)
            for j in range(NX):
                picked[j, at, n : n + 512] = picked_rows[j * CAP : (j + 1) * CAP]
                both = jnp.maximum(size[j * CAP : j * CAP + 8], size[j * CAP + 8 : (j + 1) * CAP])
                peak[j, :, n : n + 512] = jnp.maximum(peak[j, :, n : n + 512], both)

    local[3].wait()
    pick(c, z, 0)
    mate_meta(mate_c, 0, 0, z).wait_recv()
    mate(mate_c, 0, 0, z).wait_recv()
    pick(mate_c, z, 1)

    over_rows = (((0,), (0,)), ((), ()))

    def project(i, start, count):
        j = (x + i + 1) % NX

        def tile(n, carry):
            n = pl.ds(pl.multiple_of(n * 256, 256), 256)
            proj[0:count, n] = jnp.dot(
                picked[j, start : start + count, :], weights[j, :, n], preferred_element_type=F32
            )
            return carry

        lax.fori_loop(0, 2 * FWIN // 256, tile, 0)

        def gate(t, carry):
            m = pl.ds(pl.multiple_of(t * 64, 64), 64)
            g = proj[m, 0:FWIN]
            h = (g / (1.0 + jnp.exp(-g)) * proj[m, FWIN : 2 * FWIN]).astype(BF16)
            s = row_share[j, pl.ds(pl.multiple_of(start + t * 64, 64), 64), :]
            w = h.astype(F32) * jnp.concatenate([s] * (FWIN // BLK), axis=1)
            high = w.astype(BF16)
            hid[m, :] = h
            wtd[m, 0:FWIN] = high
            wtd[m, FWIN : 2 * FWIN] = (w - high.astype(F32)).astype(BF16)
            return carry

        lax.fori_loop(0, count // 64, gate, 0)
        h = hid[0:count, :]
        g = lax.dot_general(h, wtd[0:count, 0:FWIN], over_rows, preferred_element_type=F32)
        g = g + lax.dot_general(
            h, wtd[0:count, FWIN : 2 * FWIN], over_rows, preferred_element_type=F32
        )
        if start == 0:
            gram[i] = g
        else:
            gram[i] = gram[i] + g

    def mate_picks(s):
        for d in (0, 1):
            o = origin(d, s)
            mate_meta(mate_c, s, d, o).wait_recv()
            mate(mate_c, s, d, o).wait_recv()
            pick(mate_c, o, 4 * s + d)

    def relayed(ks):
        for k in ks:
            for d in (0, 1):
                second_relay(k, d, places[k], 2).wait_recv()

    def ring_step(s, carry):
        for h in range(NH):
            for d in (0, 1):
                o = origin(d, s)
                if h == 0:
                    ring_meta(d, s - 1, o).wait_recv()

                    @pl.when((s < HOPS - 1) | (d == 0))
                    def _():
                        ring_meta(d, s, o).start()

                    mate_meta(c, s, d, o).start()
                ring(d, s - 1, h, o).wait_recv()

                @pl.when((s < HOPS - 1) | (d == h % 2))
                def _():
                    ring(d, s, h, o).start()

                if h == NH - 1:
                    mate(c, s, d, o).start()

            if h == 0:

                @pl.when(s >= 2)
                def _():
                    mate_picks(s - 1)

                @pl.when(s == HOPS - 2)
                def _():
                    relayed((1, 2))

                @pl.when(s == HOPS - 1)
                def _():
                    relayed((3,))

                @pl.when(s >= HOPS - 2)
                def _():
                    project(s - (HOPS - 2), 0, EARLY[0])

        @pl.when(s == 2)
        def _():
            for d in (0, 1):
                first(d, sides[d]).wait_recv()
                first_relay(d, sides[d]).start()
            for k in (1, 2):
                for d in (0, 1):
                    second(k, d, places[k], 0).start()

        @pl.when(s == 3)
        def _():
            for d in (0, 1):
                first_relay(d, 2).wait_recv()
                second(0, d, 0, sides[d]).wait_recv()
                second_relay(0, d, 0, sides[d]).start()
            for d in (0, 1):
                second(3, d, 2, 0).start()

        @pl.when(s == 4)
        def _():
            for k in (1, 2):
                for d in (0, 1):
                    second(k, d, places[k], sides[d]).wait_recv()
                    second_relay(k, d, places[k], sides[d]).start()

        @pl.when(s == 5)
        def _():
            for d in (0, 1):
                second(3, d, 2, sides[d]).wait_recv()
                second_relay(3, d, 2, sides[d]).start()

        for d in (0, 1):
            pick(c, origin(d, s), 4 * s - 2 + d)

        @pl.when(s == HOPS - 3)
        def _():
            relayed((0,))

        @pl.when((s == HOPS - 3) | (s == HOPS - 2))
        def _():
            project(HOPS - s, 0, EARLY[0])

        @pl.when(s == HOPS - 1)
        def _():
            def middle(i, carry):
                project(i, EARLY[0], EARLY[1] - EARLY[0])
                return carry

            lax.fori_loop(0, NX, middle, 0)

        return carry

    lax.fori_loop(1, HOPS, ring_step, 0)


    far = (z + HOPS) % NZ
    last = HOPS - 1
    ring_meta(0, last, far).wait_recv()
    mate_meta(c, HOPS, 0, far).start()
    for h in range(NH):
        ring(h % 2, last, h, far).wait_recv()
        mate(c, HOPS, h, far, rows_of(h)).start()
    mate_picks(last)
    pick(c, far, NB - 2)
    mate_meta(mate_c, HOPS, 0, far).wait_recv()
    for h in range(NH):
        mate(mate_c, HOPS, h, far, rows_of(h)).wait_recv()
    pick(mate_c, far, NB - 1)

    width = FWIN // (2 * NY)
    f = x * (1 - c) + y * c
    g = y * (1 - c) + x * c

    def to_x(i):
        return send(part_max.at[i], got_x_max.at[i], mx_s.at[i], mx_r.at[i], dev(dx=i + 1))

    for i in range(NX):
        top = jnp.max(peak[(x + i + 1) % NX], axis=0, keepdims=True)
        for r in range(D // BLK):
            part_max[i, r : r + 1, :] = top[:, r * BLK : (r + 1) * BLK]

    def to_1(i):
        return send(part.at[(f + i + 1) % NX], got_1.at[i], g1_s.at[i], g1_r.at[i],
                    first_dev(i + 1))

    def piece_1(i, k):
        pair = pl.ds((x + i + 1) % NX * 2, 2)
        return send(part.at[(f + k + 1) % NX, pair], got_1.at[k, pair], p1_s.at[i, k],
                    p1_r.at[i, k], first_dev(k + 1))

    def both(act, i):
        if i < NX - 1:

            @pl.when(c == 0)
            def _():
                act(to_1(i))

        @pl.when(c == 1)
        def _():
            for k in (1, 0, 2):
                act(piece_1(i, k))

    for i in range(NX):
        project(i, EARLY[1], ROWS - EARLY[1])
        if i > 0:
            both(lambda copy: copy.start(), i - 1)
        else:
            for k in range(NX - 1):
                to_x(k).start()
        j = (x + i + 1) % NX
        for q in range(2 * NY):
            piece = gram[i, q * width : (q + 1) * width, :].astype(BF16)
            part[j * (1 - c) + q // 2 * c, q * (1 - c) + (2 * j + q % 2) * c] = piece
    both(lambda copy: copy.start(), NX - 1)
    for i in range(NX - 1):
        to_x(i).wait_recv()
    slice_max[...] = jnp.maximum(
        jnp.maximum(part_max[NX - 1], got_x_max[0]), jnp.maximum(got_x_max[1], got_x_max[2])
    )
    got_y_max[c, y] = slice_max[...]
    for i in range(NX):
        both(lambda copy: copy.wait_recv(), i)
    for q in range(2 * NY):
        total = part[f, q].astype(F32)
        for i in range(NX - 1):
            total = total + got_1[i, q].astype(F32)
        slices[q] = total.astype(BF16)
    got_2[c, g] = slices[2 * g + c]

    def to_y(k):
        step, core = k // 2, (c if k % 2 == 0 else mate_c)
        here = dev(dx=step * c, dy=step * (1 - c), core=core)
        return (
            send(slices.at[2 * ((g + step) % NX) + core], got_2.at[c, g], g2_s.at[k - 1],
                 g2_r.at[k - 1], here),
            send(slice_max, got_y_max.at[c, y], my_s.at[k - 1], my_r.at[k - 1],
                 dev(dy=step, core=core)),
        )

    def from_y(k):
        step, core = k // 2, (c if k % 2 == 0 else mate_c)
        src = ((g if k % 2 == 0 else f) - step) % NX
        here = dev(dx=step * c, dy=step * (1 - c), core=core)
        return (
            send(slices.at[0], got_2.at[core, src], g2_s.at[k - 1], g2_r.at[k - 1], here),
            send(slice_max, got_y_max.at[core, (y - step) % NY], my_s.at[k - 1], my_r.at[k - 1],
                 dev(dy=step, core=core)),
        )

    for k in range(1, 2 * NY):
        for copy in to_y(k):
            copy.start()

    for d in (0, 1):
        first(d, 0).wait_send()
        first_relay(d, sides[d]).wait_send()
        for k in range(4):
            second(k, d, places[k], 0).wait_send()
            second_relay(k, d, places[k], sides[d]).wait_send()
    swap.wait_send()
    mate_meta(c, 0, 0, z).wait_send()
    mate(c, 0, 0, z, None, tok).wait_send()
    for d in (0, 1):
        ring_meta(d, 0, z).wait_send()
        for h in range(NH):
            ring(d, 0, h, z, tok.at[rows_of(h)]).wait_send()

    def drain(s, carry):
        for d in (0, 1):
            o = origin(d, s)
            mate_meta(c, s, d, o).wait_send()
            mate(c, s, d, o).wait_send()

            @pl.when((s < HOPS - 1) | (d == 0))
            def _():
                ring_meta(d, s, o).wait_send()

            for h in range(NH):

                @pl.when((s < HOPS - 1) | (d == h % 2))
                def _():
                    ring(d, s, h, o).wait_send()

        return carry

    lax.fori_loop(1, HOPS, drain, 0)
    mate_meta(c, HOPS, 0, far).wait_send()
    for h in range(NH):
        mate(c, HOPS, h, far, rows_of(h)).wait_send()
    for i in range(NX - 1):
        to_x(i).wait_send()
    for i in range(NX):
        both(lambda copy: copy.wait_send(), i)

    for k in range(1, 2 * NY):
        for copy in from_y(k):
            copy.wait_recv()
    row = lax.broadcasted_iota(jnp.int32, (D // BLK, BLK), 0)
    for p in (0, 1):
        total = got_2[p, 0].astype(F32)
        top = got_y_max[p, 0]
        for k in range(1, NY):
            total = total + got_2[p, k].astype(F32)
            top = jnp.maximum(top, got_y_max[p, k])
        gram_out[p] = total * NORM
        for r in (0, 1):
            here = jnp.where(row == 2 * seq + r, top, 0.0)
            max_out[p : p + 1, r * BLK : (r + 1) * BLK] = jnp.max(here, axis=0, keepdims=True)
    for k in range(1, 2 * NY):
        for copy in to_y(k):
            copy.wait_send()


def body(tokens, routes, gate_shares, gate_up):
    dma = pltpu.SemaphoreType.DMA
    width = FWIN // (2 * NY)
    pairs = [
        (2, HOPS, NH), (2, HOPS), (HOPS + 1, NH), (HOPS + 1, 2), (), (2,), (2,), (4, 2), (4, 2),
        (NX - 1,), (NX, NX - 1), (NX - 1,), (2 * NY - 1,), (2 * NY - 1,),
    ]
    sems = [dma((4,))]
    for shape in pairs:
        sems += [dma(shape), dma(shape)]
    return pl.pallas_call(
        kernel,
        out_shape=(
            jax.ShapeDtypeStruct((2, width, FWIN), F32),
            jax.ShapeDtypeStruct((2, D // (2 * NY)), F32),
        ),
        in_specs=[pl.BlockSpec(memory_space=pl.ANY)] * 4,
        out_specs=(
            pl.BlockSpec(memory_space=pltpu.VMEM),
            pl.BlockSpec(memory_space=pltpu.VMEM),
        ),
        scratch_shapes=[
            pltpu.VMEM((2, NZ, BLK, D), BF16),
            pltpu.VMEM((2, NZ, 2 * TOP, BLK), jnp.int32),
            pltpu.VMEM((NX, ROWS, D), BF16),
            pltpu.VMEM((NX, ROWS, BLK), F32),
            pltpu.VMEM((NX, 8, D), F32),
            pltpu.VMEM((NX, D, 2 * FWIN), BF16),
            pltpu.VMEM((BLK, BLK), BF16),
            pltpu.VMEM((EARLY[0], 2 * FWIN), F32),
            pltpu.VMEM((EARLY[0], FWIN), BF16),
            pltpu.VMEM((EARLY[0], 2 * FWIN), BF16),
            pltpu.VMEM((NX, FWIN, FWIN), F32),
            pltpu.VMEM((NX, 2 * NY, width, FWIN), BF16),
            pltpu.VMEM((NX, D // BLK, BLK), F32),
            pltpu.VMEM((NX - 1, 2 * NY, width, FWIN), BF16),
            pltpu.VMEM((NX - 1, D // BLK, BLK), F32),
            pltpu.VMEM((2 * NY, width, FWIN), BF16),
            pltpu.VMEM((D // BLK, BLK), F32),
            pltpu.VMEM((2, NY, width, FWIN), BF16),
            pltpu.VMEM((2, NY, D // BLK, BLK), F32),
            *sems,
        ],
        compiler_params=pltpu.CompilerParams(
            collective_id=0, has_side_effects=True, vmem_limit_bytes=60 * 1024 * 1024
        ),
    )(tokens, routes.T, gate_shares.T, gate_up)


def solution(mesh):
    return jax.shard_map(
        body,
        mesh=mesh,
        in_specs=(
            P(("seq", "expert"), None),
            P(("seq", "expert"), None),
            P(("seq", "expert"), None),
            P("expert", "seq", None),
        ),
        out_specs=(P("expert", "seq", None), P("expert", "seq")),
        check_vma=False,
    )
```

time: 142 us -> 131 us (0.923)
  Pallas kernels: 138 us -> 128 us
    pallas_call x1, Pallas kernels: 138 us -> 128 us  [body(): pl.pallas_call(kernel, out_shape=(jax.ShapeDtypeStruct((2, width, FWIN),...]
where the time goes in v2:
time: 131 us
  Pallas kernels  128 us (98%)
  local copies, waits for them, and re-layouts  2.16 us (2%)
    pallas_call x1, Pallas kernels, body(): pl.pallas_call(kernel, out_shape=(jax.ShapeDtypeStruct((2, width, FWIN),...  128 us

profile of v2, /device:TPU:1, one launch (start us, length us, event | category | flops | bytes accessed | tf_op | source)
XLA Modules:
  0.0 130.9 jit_solution(11178033281128980474)
XLA Ops:
  0.6 128.1 %shard_map.59 = (f32[2,48,384]{2,1,0:T(8,128)}, f32[2,256]{1,0:T(2,128)}) custom-call(bf16[128,2048]{1,0:T(8,128)(2,1)} %tok.1, s32[8,128]{1,0:T(8,128)} %bitcast.2, s32[8,128]{1,0:T(8,128)} %bitcast.3, bf16[2,256,768]{2,1,0:T(8,128)(2,1)} %wgt.1), custom_call_target="tpu_custom_call" | custom-call | tf_op jit(solution)/shard_map/pallas_call | solution.py:496
  128.8 0.0 copy-start
  128.8 1.6 %copy.8 = f32[2,48,384]{2,1,0:T(8,128)} copy(f32[2,48,384]{2,1,0:T(8,128)} %get-tuple-element.4) | data formatting | bytes 294912
  130.3 0.0 copy-done
  130.3 0.6 copy.9
Async XLA Ops:
  128.8 1.6 %copy-start = (f32[2,256]{1,0:T(2,128)S(1)}, f32[2,256]{1,0:T(2,128)}, u32[]{:S(2)}) copy-start(f32[2,256]{1,0:T(2,128)} %get-tuple-element.5) | copy-start | bytes 6148

commit v3 on v2

--- a/solution.py
+++ b/solution.py
@@ -20,7 +20,7 @@
 DSEQ = D // (2 * NY)
 NB = 2 * NZ
 ROWS = NB * CAP
-EARLY = (256, 384)
+EARLY = 320
 MESH = pl.DeviceIdType.MESH
 NORM = EXPERTS / (BLK * 2 * NY * NX * NZ * TOP)
 F32 = jnp.float32
@@ -73,6 +73,9 @@
     def origin(d, s):
         return (z - s) % NZ if d == 0 else (z + s) % NZ
 
+    def order(d, n):
+        return n if d == 0 else NH - 1 - n
+
     def rows_of(h):
         return pl.ds(h * PIECE, PIECE)
 
@@ -129,7 +132,8 @@
 
     swap = send(wgt.at[mate_c], weights.at[x, own_rows], swap_s, swap_r, dev(core=mate_c))
     for d in (0, 1):
-        for h in range(NH):
+        for n in range(NH):
+            h = order(d, n)
             ring(d, 0, h, z, tok.at[rows_of(h)]).start()
     swap.start()
     local[0].wait()
@@ -148,7 +152,10 @@
     slot = lax.broadcasted_iota(jnp.int32, (CAP, BLK), 0).astype(F32)
     expert_id = z * 2 * NX + c + 2 * lax.broadcasted_iota(jnp.int32, (8, BLK), 0)
 
-    def pick(owner, o, b):
+    def slots_of(b):
+        return pl.ds(b * CAP if isinstance(b, int) else pl.multiple_of(b * CAP, CAP), CAP)
+
+    def choose(owner, o, b):
         info = metas[owner, o]
         named = jnp.zeros((8, BLK), F32)
         share = jnp.zeros((8, BLK), jnp.int32)
@@ -159,14 +166,17 @@
         share = share.astype(F32)
         rank = jnp.dot(named.astype(BF16), upper[...], preferred_element_type=F32)
         rank = jnp.where(named > 0.5, rank, -1.0)
-        at = pl.ds(pl.multiple_of(b * CAP, CAP), CAP)
+        at = slots_of(b)
         chosen = []
         for j in range(NX):
             one = jnp.where(rank[j : j + 1, :] == slot, 1.0, 0.0)
             chosen.append(one)
             col = jnp.sum(one * share[j : j + 1, :], axis=1, keepdims=True) * (1.0 / 65536.0)
             row_share[j, at, :] = jnp.broadcast_to(col, (CAP, BLK))
-        chosen = jnp.concatenate(chosen, axis=0).astype(BF16)
+        return jnp.concatenate(chosen, axis=0).astype(BF16)
+
+    def gather(chosen, owner, o, b):
+        at = slots_of(b)
         for n in range(0, D, 512):
             got = jnp.dot(chosen, toks[owner, o, :, n : n + 512], preferred_element_type=F32)
             picked_rows = got.astype(BF16)
@@ -176,43 +186,54 @@
                 both = jnp.maximum(size[j * CAP : j * CAP + 8], size[j * CAP + 8 : (j + 1) * CAP])
                 peak[j, :, n : n + 512] = jnp.maximum(peak[j, :, n : n + 512], both)
 
+    def pick(owner, o, b):
+        gather(choose(owner, o, b), owner, o, b)
+
     local[3].wait()
     pick(c, z, 0)
     mate_meta(mate_c, 0, 0, z).wait_recv()
     mate(mate_c, 0, 0, z).wait_recv()
     pick(mate_c, z, 1)
 
-    over_rows = (((0,), (0,)), ((), ()))
-
-    def project(i, start, count):
+    def project(i, start, count, flat=False):
         j = (x + i + 1) % NX
 
+        def loop(n, step):
+            if flat:
+                for t in range(n):
+                    step(t, 0)
+            else:
+                lax.fori_loop(0, n, step, 0)
+
         def tile(n, carry):
-            n = pl.ds(pl.multiple_of(n * 256, 256), 256)
+            n = pl.ds(n * 256 if flat else pl.multiple_of(n * 256, 256), 256)
             proj[0:count, n] = jnp.dot(
                 picked[j, start : start + count, :], weights[j, :, n], preferred_element_type=F32
             )
             return carry
 
-        lax.fori_loop(0, 2 * FWIN // 256, tile, 0)
+        loop(2 * FWIN // 256, tile)
 
         def gate(t, carry):
-            m = pl.ds(pl.multiple_of(t * 64, 64), 64)
+            m = pl.ds(t * 64 if flat else pl.multiple_of(t * 64, 64), 64)
             g = proj[m, 0:FWIN]
             h = (g / (1.0 + jnp.exp(-g)) * proj[m, FWIN : 2 * FWIN]).astype(BF16)
-            s = row_share[j, pl.ds(pl.multiple_of(start + t * 64, 64), 64), :]
+            at = start + t * 64
+            s = row_share[j, pl.ds(at if flat else pl.multiple_of(at, 64), 64), :]
             w = h.astype(F32) * jnp.concatenate([s] * (FWIN // BLK), axis=1)
             high = w.astype(BF16)
+            low = count + t * 64
             hid[m, :] = h
-            wtd[m, 0:FWIN] = high
-            wtd[m, FWIN : 2 * FWIN] = (w - high.astype(F32)).astype(BF16)
+            wtd[m, :] = high
+            wtd[pl.ds(low if flat else pl.multiple_of(low, 64), 64), :] = (
+                w - high.astype(F32)
+            ).astype(BF16)
             return carry
 
-        lax.fori_loop(0, count // 64, gate, 0)
-        h = hid[0:count, :]
-        g = lax.dot_general(h, wtd[0:count, 0:FWIN], over_rows, preferred_element_type=F32)
-        g = g + lax.dot_general(
-            h, wtd[0:count, FWIN : 2 * FWIN], over_rows, preferred_element_type=F32
+        loop(count // 64, gate)
+        h = hid[0:count, :].T
+        g = jnp.dot(
+            jnp.concatenate([h, h], axis=1), wtd[0 : 2 * count, :], preferred_element_type=F32
         )
         if start == 0:
             gram[i] = g
@@ -232,10 +253,11 @@
                 second_relay(k, d, places[k], 2).wait_recv()
 
     def ring_step(s, carry):
-        for h in range(NH):
+        for n in range(NH):
             for d in (0, 1):
                 o = origin(d, s)
-                if h == 0:
+                h = order(d, n)
+                if n == 0:
                     ring_meta(d, s - 1, o).wait_recv()
 
                     @pl.when((s < HOPS - 1) | (d == 0))
@@ -245,14 +267,18 @@
                     mate_meta(c, s, d, o).start()
                 ring(d, s - 1, h, o).wait_recv()
 
-                @pl.when((s < HOPS - 1) | (d == h % 2))
-                def _():
+                if n < NH // 2:
                     ring(d, s, h, o).start()
-
-                if h == NH - 1:
+                else:
+
+                    @pl.when(s < HOPS - 1)
+                    def _():
+                        ring(d, s, h, o).start()
+
+                if n == NH - 1:
                     mate(c, s, d, o).start()
 
-            if h == 0:
+            if n == 0:
 
                 @pl.when(s >= 2)
                 def _():
@@ -268,7 +294,7 @@
 
                 @pl.when(s >= HOPS - 2)
                 def _():
-                    project(s - (HOPS - 2), 0, EARLY[0])
+                    project(s - (HOPS - 2), 0, EARLY)
 
         @pl.when(s == 2)
         def _():
@@ -310,15 +336,7 @@
 
         @pl.when((s == HOPS - 3) | (s == HOPS - 2))
         def _():
-            project(HOPS - s, 0, EARLY[0])
-
-        @pl.when(s == HOPS - 1)
-        def _():
-            def middle(i, carry):
-                project(i, EARLY[0], EARLY[1] - EARLY[0])
-                return carry
-
-            lax.fori_loop(0, NX, middle, 0)
+            project(HOPS - s, 0, EARLY)
 
         return carry
 
@@ -327,17 +345,21 @@
 
     far = (z + HOPS) % NZ
     last = HOPS - 1
+    mate_picks(last)
     ring_meta(0, last, far).wait_recv()
     mate_meta(c, HOPS, 0, far).start()
-    for h in range(NH):
-        ring(h % 2, last, h, far).wait_recv()
-        mate(c, HOPS, h, far, rows_of(h)).start()
-    mate_picks(last)
-    pick(c, far, NB - 2)
+    own_far = choose(c, far, NB - 2)
     mate_meta(mate_c, HOPS, 0, far).wait_recv()
+    mate_far = choose(mate_c, far, NB - 1)
+    for n in range(NH // 2):
+        for d in (0, 1):
+            h = order(d, n)
+            ring(d, last, h, far).wait_recv()
+            mate(c, HOPS, h, far, rows_of(h)).start()
+    gather(own_far, c, far, NB - 2)
     for h in range(NH):
         mate(mate_c, HOPS, h, far, rows_of(h)).wait_recv()
-    pick(mate_c, far, NB - 1)
+    gather(mate_far, mate_c, far, NB - 1)
 
     width = FWIN // (2 * NY)
     f = x * (1 - c) + y * c
@@ -373,7 +395,7 @@
                 act(piece_1(i, k))
 
     for i in range(NX):
-        project(i, EARLY[1], ROWS - EARLY[1])
+        project(i, EARLY, ROWS - EARLY, flat=True)
         if i > 0:
             both(lambda copy: copy.start(), i - 1)
         else:
@@ -392,12 +414,13 @@
     got_y_max[c, y] = slice_max[...]
     for i in range(NX):
         both(lambda copy: copy.wait_recv(), i)
-    for q in range(2 * NY):
-        total = part[f, q].astype(F32)
-        for i in range(NX - 1):
-            total = total + got_1[i, q].astype(F32)
-        slices[q] = total.astype(BF16)
-    got_2[c, g] = slices[2 * g + c]
+    def add_up(step):
+        for q in (0, 1):
+            at = 2 * ((g + step) % NX) + q
+            total = part[f, at].astype(F32)
+            for i in range(NX - 1):
+                total = total + got_1[i, at].astype(F32)
+            slices[at] = total.astype(BF16)
 
     def to_y(k):
         step, core = k // 2, (c if k % 2 == 0 else mate_c)
@@ -420,8 +443,15 @@
         )
 
     for k in range(1, 2 * NY):
-        for copy in to_y(k):
-            copy.start()
+        to_y(k)[1].start()
+    add_up(2)
+    for step in (1, 3, 0):
+        add_up(step)
+        before = {1: 2, 3: 1, 0: 3}[step]
+        for k in (2 * before, 2 * before + 1):
+            to_y(k)[0].start()
+    got_2[c, g] = slices[2 * g + c]
+    to_y(1)[0].start()
 
     for d in (0, 1):
         first(d, 0).wait_send()
@@ -449,7 +479,7 @@
 
             for h in range(NH):
 
-                @pl.when((s < HOPS - 1) | (d == h % 2))
+                @pl.when((s < HOPS - 1) | (d == h // (NH // 2)))
                 def _():
                     ring(d, s, h, o).wait_send()
 
@@ -512,9 +542,9 @@
             pltpu.VMEM((NX, 8, D), F32),
             pltpu.VMEM((NX, D, 2 * FWIN), BF16),
             pltpu.VMEM((BLK, BLK), BF16),
-            pltpu.VMEM((EARLY[0], 2 * FWIN), F32),
-            pltpu.VMEM((EARLY[0], FWIN), BF16),
-            pltpu.VMEM((EARLY[0], 2 * FWIN), BF16),
+            pltpu.VMEM((EARLY, 2 * FWIN), F32),
+            pltpu.VMEM((EARLY, FWIN), BF16),
+            pltpu.VMEM((2 * EARLY, FWIN), BF16),
             pltpu.VMEM((NX, FWIN, FWIN), F32),
             pltpu.VMEM((NX, 2 * NY, width, FWIN), BF16),
             pltpu.VMEM((NX, D // BLK, BLK), F32),

time: 131 us -> 129 us (0.985)
  Pallas kernels: 128 us -> 126 us
    pallas_call x1, Pallas kernels: 128 us -> 126 us  [body(): pl.pallas_call(kernel, out_shape=(jax.ShapeDtypeStruct((2, width, FWIN),...]
where the time goes in v3:
time: 129 us
  Pallas kernels  126 us (98%)
  local copies, waits for them, and re-layouts  2.16 us (2%)
    pallas_call x1, Pallas kernels, body(): pl.pallas_call(kernel, out_shape=(jax.ShapeDtypeStruct((2, width, FWIN),...  126 us

profile of v3, /device:TPU:1, one launch (start us, length us, event | category | flops | bytes accessed | tf_op | source)
XLA Modules:
  0.0 128.8 jit_solution(13409457258408396539)
XLA Ops:
  0.6 125.9 %shard_map.59 = (f32[2,48,384]{2,1,0:T(8,128)}, f32[2,256]{1,0:T(2,128)}) custom-call(bf16[128,2048]{1,0:T(8,128)(2,1)} %tok.1, s32[8,128]{1,0:T(8,128)} %bitcast.2, s32[8,128]{1,0:T(8,128)} %bitcast.3, bf16[2,256,768]{2,1,0:T(8,128)(2,1)} %wgt.1), custom_call_target="tpu_custom_call" | custom-call | tf_op jit(solution)/shard_map/pallas_call | solution.py:526
  126.6 0.0 copy-start
  126.6 1.6 %copy.8 = f32[2,48,384]{2,1,0:T(8,128)} copy(f32[2,48,384]{2,1,0:T(8,128)} %get-tuple-element.4) | data formatting | bytes 294912
  128.2 0.0 copy-done
  128.2 0.6 copy.9
Async XLA Ops:
  126.6 1.6 %copy-start = (f32[2,256]{1,0:T(2,128)S(1)}, f32[2,256]{1,0:T(2,128)}, u32[]{:S(2)}) copy-start(f32[2,256]{1,0:T(2,128)} %get-tuple-element.5) | copy-start | bytes 6148

commit v4 on v3

--- a/solution.py
+++ b/solution.py
@@ -394,10 +394,11 @@
             for k in (1, 0, 2):
                 act(piece_1(i, k))
 
-    for i in range(NX):
+    far_first = (1, 0, 2, 3)
+    for n, i in enumerate(far_first):
         project(i, EARLY, ROWS - EARLY, flat=True)
-        if i > 0:
-            both(lambda copy: copy.start(), i - 1)
+        if n > 0:
+            both(lambda copy: copy.start(), far_first[n - 1])
         else:
             for k in range(NX - 1):
                 to_x(k).start()

time: 129 us -> 128 us (level)
  no operation moved by 1% of the time
where the time goes in v4:
time: 128 us
  Pallas kernels  125 us (98%)
  local copies, waits for them, and re-layouts  2.16 us (2%)
    pallas_call x1, Pallas kernels, body(): pl.pallas_call(kernel, out_shape=(jax.ShapeDtypeStruct((2, width, FWIN),...  125 us

profile of v4, /device:TPU:1, one launch (start us, length us, event | category | flops | bytes accessed | tf_op | source)
XLA Modules:
  0.0 128.0 jit_solution(15518485969119267113)
XLA Ops:
  0.6 125.2 %shard_map.59 = (f32[2,48,384]{2,1,0:T(8,128)}, f32[2,256]{1,0:T(2,128)}) custom-call(bf16[128,2048]{1,0:T(8,128)(2,1)} %tok.1, s32[8,128]{1,0:T(8,128)} %bitcast.2, s32[8,128]{1,0:T(8,128)} %bitcast.3, bf16[2,256,768]{2,1,0:T(8,128)(2,1)} %wgt.1), custom_call_target="tpu_custom_call" | custom-call | tf_op jit(solution)/shard_map/pallas_call | solution.py:527
  125.8 0.0 copy-start
  125.8 1.6 %copy.8 = f32[2,48,384]{2,1,0:T(8,128)} copy(f32[2,48,384]{2,1,0:T(8,128)} %get-tuple-element.4) | data formatting | bytes 294912
  127.4 0.0 copy-done
  127.4 0.6 copy.9
Async XLA Ops:
  125.8 1.6 %copy-start = (f32[2,256]{1,0:T(2,128)S(1)}, f32[2,256]{1,0:T(2,128)}, u32[]{:S(2)}) copy-start(f32[2,256]{1,0:T(2,128)} %get-tuple-element.5) | copy-start | bytes 6148
